TPU v7x, 256 devices: a whole 4x4x8 slice. The times are simulated.
256 devices in a mesh: wide: 64 (over y, z, core), narrow: 4 (over x).
Axes of the slice: x: 4, y: 4, z: 8, core: 2. Of those that a mesh axis runs over, the one named last changes fastest.
Arguments:
- residual_in: bfloat16 [128, 7168], P('wide', 'narrow'), may hold values from -2 to 2
- query_nope: bfloat16 [128, 64, 128], P('wide', 'narrow'), may hold values from -6 to 6
- query_rope: bfloat16 [128, 64, 64], P('wide', 'narrow'), may hold values from -8 to 8
- absorb_key: bfloat16 [64, 128, 512], P('narrow'), may hold values from -0.5 to 0.5
- absorb_value: bfloat16 [64, 512, 128], P('narrow'), may hold values from -0.25 to 0.25
- latent_cache: bfloat16 [128, 2048, 576], P('wide'), may hold values from -8 to 8
- cache_lengths: int32 [128], P('wide'), may hold values from 256 to 2048, as said below
- slot_rows: int32 [128], replicated, may hold values from 0 to 127, each once
- out_proj: bfloat16 [8192, 7168], P('wide', 'narrow'), may hold values from -0.0625 to 0.0625
- norm_gain: bfloat16 [7168], P('narrow'), may hold values from 0.25 to 1.75
- gate_weight: bfloat16 [7168, 18432], P('narrow', 'wide'), may hold values from -0.0625 to 0.0625
- up_weight: bfloat16 [7168, 18432], P('narrow', 'wide'), may hold values from -0.0625 to 0.0625
- down_weight: bfloat16 [18432, 7168], P('wide', 'narrow'), may hold values from -0.046875 to 0.046875
Outputs:
- residual_out: bfloat16 [128, 7168], P('wide', 'narrow')
Inputs may be any that keep to these rules, and one draw needn't show every extreme that they name: `cache_lengths`: every slot has at least 256 live positions; in every draw some slot is full. `slot_rows`: each batch row is named by exactly one slot.
All inputs are finite; a program needn't handle non-finite values.
Results may differ from a plain program's by a relative error of at most 0.009.
Values may be sent and summed in bfloat16 or wider, within the bound.
A program may use at most 64 MiB of HBM per device.

v0:
```python
import math
import jax
import jax.numpy as jnp
from jax import lax
from jax.sharding import PartitionSpec as P

D = 7168


def shards(
    residual_in,
    query_nope,
    query_rope,
    absorb_key,
    absorb_value,
    latent_cache,
    cache_lengths,
    slot_rows,
    out_proj,
    norm_gain,
    gate_weight,
    up_weight,
    down_weight,
):
    slot_count = latent_cache.shape[0]
    head_size = query_nope.shape[2]
    latent_width = absorb_key.shape[2]
    group_index = lax.axis_index("wide")
    packed_queries = jnp.concatenate([query_nope, query_rope], axis=2)
    gathered = lax.all_gather(packed_queries, "wide", axis=0, tiled=True)
    my_rows = lax.dynamic_slice_in_dim(slot_rows, group_index * slot_count, slot_count)
    selected = jnp.take(gathered, my_rows, axis=0)
    query_latent = jnp.einsum(
        "rhd,hdc->rhc", selected[:, :, :head_size], absorb_key, preferred_element_type=jnp.float32
    ).astype(jnp.bfloat16)
    full_query = jnp.concatenate([query_latent, selected[:, :, head_size:]], axis=2)
    scale = 1.0 / math.sqrt(full_query.shape[2] - latent_width + head_size)
    scores = (
        jnp.einsum("rhc,rtc->rht", full_query, latent_cache, preferred_element_type=jnp.float32)
        * scale
    )
    positions = jnp.arange(latent_cache.shape[1], dtype=jnp.int32)
    live = positions[None, None, :] < cache_lengths[:, None, None]
    scores = jnp.where(live, scores, -jnp.inf)
    highest = jnp.max(scores, axis=2, keepdims=True)
    weights = jnp.where(live, jnp.exp(scores - highest), 0.0)
    probs = (weights / jnp.sum(weights, axis=2, keepdims=True)).astype(jnp.bfloat16)
    context = jnp.einsum("rht,rtc->rhc", probs, latent_cache, preferred_element_type=jnp.float32)
    context = context[:, :, :latent_width].astype(jnp.bfloat16)
    heads_out = jnp.einsum(
        "rhc,hcd->rhd", context, absorb_value, preferred_element_type=jnp.float32
    ).astype(jnp.bfloat16)
    every_head = lax.all_gather(heads_out, "narrow", axis=1, tiled=True)
    flat_heads = every_head.reshape(slot_count, -1)
    head_columns = lax.all_to_all(flat_heads, "wide", split_axis=1, concat_axis=0, tiled=True)
    inverse = jnp.argsort(slot_rows)
    attention = lax.psum_scatter(
        jnp.dot(
            jnp.take(head_columns, inverse, axis=0), out_proj, preferred_element_type=jnp.float32
        ),
        "wide",
        scatter_dimension=0,
        tiled=True,
    )
    middle = residual_in.astype(jnp.float32) + attention
    square_sum = lax.psum(jnp.sum(middle * middle, axis=1), "narrow")
    normed = (
        middle * lax.rsqrt(square_sum / D + 1e-06)[:, None] * norm_gain.astype(jnp.float32)
    ).astype(jnp.bfloat16)
    hidden_cols = gate_weight.shape[1]
    row_piece = lax.all_gather(normed, "wide", axis=0, tiled=True)
    local_terms = jnp.concatenate(
        [
            jnp.dot(row_piece, gate_weight, preferred_element_type=jnp.float32),
            jnp.dot(row_piece, up_weight, preferred_element_type=jnp.float32),
        ],
        axis=1,
    )
    summed = lax.psum(local_terms, "narrow")
    hidden = (jax.nn.silu(summed[:, :hidden_cols]) * summed[:, hidden_cols:]).astype(jnp.bfloat16)
    ffn_total = lax.psum_scatter(
        jnp.dot(hidden, down_weight, preferred_element_type=jnp.float32),
        "wide",
        scatter_dimension=0,
        tiled=True,
    )
    return (middle + ffn_total).astype(jnp.bfloat16)


def solution(mesh):
    in_specs = (
        P("wide", "narrow"),
        P("wide", "narrow", None),
        P("wide", "narrow", None),
        P("narrow", None, None),
        P("narrow", None, None),
        P("wide", None, None),
        P("wide"),
        P(),
        P("wide", "narrow"),
        P("narrow"),
        P("narrow", "wide"),
        P("narrow", "wide"),
        P("wide", "narrow"),
    )
    out_specs = P("wide", "narrow")
    return jax.shard_map(shards, mesh=mesh, in_specs=in_specs, out_specs=out_specs, check_vma=False)
```

profile of v0, /device:TPU:2, one launch (start us, length us, event | category | flops | bytes accessed | tf_op | source)
XLA Modules:
  0.0 592.2 jit_solution(973563443931683544)
XLA Ops:
  6.5 0.0 copy-start
  6.5 0.9 compare_and_fusion
  7.4 0.7 pad_maximum_fusion.1
  8.2 53.8 %all_gather.9 = bf16[128,16,192]{2,1,0:T(8,128)(2,1)S(1)} all-gather(bf16[2,16,192]{2,1,0:T(8,128)(2,1)S(1)} %pad_maximum_fusion.1), channel_id=1, replica_groups=mesh['wide'=64,'narrow'=4] {'wide'}, dimensions={0}, use_global_device_ids=true | all-gather | bytes 798720 | tf_op jit(solution)/shard_map/all_gather | solution.py:30
  61.9 0.5 gather_fusion
  62.5 0.1 broadcast_select_fusion
  62.6 0.7 iota_compare_fusion
  63.3 0.0 copy-done
  63.3 0.4 fusion.21
  63.7 3.1 fusion.4
  66.8 0.2 fusion.29
  67.0 3.7 fusion.7
  70.8 0.0 copy-start.4
  70.8 0.0 copy-start.1
  70.8 0.0 copy-start.5
  70.8 0.0 copy-start.2
  70.8 0.0 copy-start.3
  70.8 2.0 fusion.5
  72.8 12.7 %all_gather.10 = bf16[2,64,128]{2,0,1:T(2,128)(2,1)} all-gather(bf16[2,16,128]{2,0,1:T(2,128)(2,1)S(1)} %fusion.5), channel_id=1, replica_groups=mesh['wide'=64,'narrow'=4] {'narrow'}, dimensions={1}, use_global_device_ids=true | all-gather | bytes 40960 | tf_op jit(solution)/shard_map/all_gather | solution.py:53
  85.6 6.7 %all-to-all-start = ((bf16[2,64,128]{2,0,1:T(2,128)(2,1)}), bf16[2,64,128]{2,0,1:T(2,128)(2,1)S(1)}, u32[]{:S(2)}, u32[]{:S(2)}) async-start(bf16[2,64,128]{2,0,1:T(2,128)(2,1)} %all_gather.10), calls=%async_computation | async-start | bytes 65536 | tf_op jit(solution)/shard_map/all_to_all | solution.py:55
  92.3 0.0 all-reduce.8.cloned.1.call-start
  92.4 0.0 copy-done.4
  92.4 2.5 sort.17
  94.9 6.9 %all-to-all-done = bf16[2,64,128]{2,0,1:T(2,128)(2,1)S(1)} async-done(((bf16[2,64,128]{2,0,1:T(2,128)(2,1)}), bf16[2,64,128]{2,0,1:T(2,128)(2,1)S(1)}, u32[]{:S(2)}, u32[]{:S(2)}) %all-to-all-start) | async-done | bytes 32800 | tf_op jit(solution)/shard_map/all_to_all | solution.py:55
  101.8 0.7 gather_fusion.1
  102.5 0.0 copy-done.1
  102.6 1.3 fusion.16
  103.9 0.0 all-reduce.8.cloned.1.call-update
  103.9 0.0 all-reduce.6.cloned.1.call-start
  103.9 0.0 copy-done.5
  103.9 0.6 dynamic-slice
  105.2 180.9 %all-reduce.8.cloned.1.call-done = f32[128,1792]{1,0:T(8,128)} async-done(((f32[128,1792]{1,0:T(8,128)}), f32[128,1792]{1,0:T(8,128)}) %all-reduce.8.cloned.1.call-update) | async-done | bytes 917520
  286.1 0.0 copy-done.2
  286.1 1.0 multiply_reduce_fusion
  287.0 0.0 copy-done.3
  287.0 8.6 %psum.14 = f32[2]{0:T(128)S(1)} all-reduce(f32[2]{0:T(128)S(1)} %multiply_reduce_fusion), channel_id=1, replica_groups=mesh['wide'=64,'narrow'=4] {'narrow'}, use_global_device_ids=true, to_apply=%region_5.6 | all-reduce | flops 2 | bytes 16 | tf_op jit(solution)/shard_map/psum | solution.py:66
  295.6 0.9 fusion.23
  296.5 48.1 %all-gather = bf16[64,2,1792]{2,1,0:T(2,128)(2,1)S(1)} all-gather(bf16[1,2,1792]{2,1,0:T(2,128)(2,1)S(1)} %fusion.23), channel_id=1, replica_groups=mesh['wide'=64,'narrow'=4] {'wide'}, dimensions={0}, use_global_device_ids=true | all-gather | bytes 465920 | tf_op jit(solution)/shard_map/all_gather | solution.py:71
  344.7 0.2 reshape.59
  344.8 1.6 fusion.31
  346.5 1.6 fusion.30
  348.1 0.7 pad_maximum_fusion
  348.9 0.0 all-reduce.6.cloned.1.call-update
  348.9 0.0 all-reduce.10.cloned.1.call-start
  349.0 42.7 %all-reduce.6.cloned.1.call-done = f32[128,576]{0,1:T(8,128)} async-done(((f32[128,576]{0,1:T(8,128)}), f32[128,576]{0,1:T(8,128)}) %all-reduce.6.cloned.1.call-update) | async-done | bytes 294928 | tf_op jit(solution)/shard_map/psum | solution.py:79
  391.7 2.8 fusion.9
  394.4 0.0 all-reduce.10.cloned.1.call-update
  394.5 189.7 %all-reduce.10.cloned.1.call-done = f32[128,1792]{1,0:T(8,128)} async-done(((f32[128,1792]{1,0:T(8,128)}), f32[128,1792]{1,0:T(8,128)}) %all-reduce.10.cloned.1.call-update) | async-done | bytes 917520
  584.2 1.5 fusion.20
  (11 shorter events, 0.1 us)
Async XLA Ops:
  6.5 56.8 %copy-start = (bf16[16,128,512]{2,1,0:T(8,128)(2,1)S(1)}, bf16[16,128,512]{2,1,0:T(8,128)(2,1)}, u32[]{:S(2)}) copy-start(bf16[16,128,512]{2,1,0:T(8,128)(2,1)} %param.16) | copy-start | bytes 6291460
  70.8 21.6 %copy-start.4 = (s32[128]{0:T(128)S(1)}, s32[128]{0:T(128)}, u32[]{:S(2)}) copy-start(s32[128]{0:T(128)} %param.20) | copy-start | bytes 1540
  70.8 31.8 %copy-start.1 = (bf16[128,1792]{1,0:T(8,128)(2,1)S(1)}, bf16[128,1792]{1,0:T(8,128)(2,1)}, u32[]{:S(2)}) copy-start(bf16[128,1792]{1,0:T(8,128)(2,1)} %param.21) | copy-start | bytes 1376260
  70.8 33.2 %copy-start.5 = (u32[256]{0:T(256)S(1)}, u32[256]{0:T(256)}, u32[]{:S(2)}) copy-start(u32[256]{0:T(256)} %constant.62) | copy-start | bytes 3076
  70.8 215.3 %copy-start.2 = (bf16[2,1792]{1,0:T(2,128)(2,1)S(1)}, bf16[2,1792]{1,0:T(2,128)(2,1)}, u32[]{:S(2)}) copy-start(bf16[2,1792]{1,0:T(2,128)(2,1)} %param.13) | copy-start | bytes 21508
  70.8 216.2 %copy-start.3 = (bf16[1792]{0:T(1024)(128)(2,1)S(1)}, bf16[1792]{0:T(1024)(128)(2,1)}, u32[]{:S(2)}) copy-start(bf16[1792]{0:T(1024)(128)(2,1)} %param.22) | copy-start | bytes 10756
  85.6 16.3 %all-to-all-start = ((bf16[2,64,128]{2,0,1:T(2,128)(2,1)}), bf16[2,64,128]{2,0,1:T(2,128)(2,1)S(1)}, u32[]{:S(2)}, u32[]{:S(2)}) async-start(bf16[2,64,128]{2,0,1:T(2,128)(2,1)} %all_gather.10), calls=%async_computation | async-start | bytes 65536 | tf_op jit(solution)/shard_map/all_to_all | solution.py:55
  92.3 193.7 %all-reduce.8.cloned.1.call-start = ((), (), s32[]{:S(2)}) async-start(), calls=%async_computation.2 | async-start | bytes 1835008
  103.9 287.8 %all-reduce.6.cloned.1.call-start = ((), (), s32[]{:S(2)}) async-start(), calls=%async_computation.1 | async-start | bytes 589824 | tf_op jit(solution)/shard_map/psum | solution.py:79
  348.9 235.3 %all-reduce.10.cloned.1.call-start = ((), (), s32[]{:S(2)}) async-start(), calls=%async_computation.3 | async-start | bytes 1835008
Sparse Core Ops, SparseCore 0:
  104.0 182.0 all-reduce.7
  349.0 42.5 all-reduce.5
  395.1 189.0 all-reduce.9
where the time goes:
time: 593 us; the launch traced here: 592 us
  waiting for transfers between devices  420 us (71%)
  blocking collectives  123 us (21%)
  matrix products  16.6 us (3%)
  between operations  13.9 us (2%)
  other arithmetic  9.27 us (2%)
  starting transfers between devices  6.87 us (1%)
    unnamed x5, waiting for transfers between devices  371 us
    all_gather x1, blocking collectives, shards(): gathered = lax.all_gather(packed_queries, 'wide', axis=0, tiled=True)  53.8 us
    all_gather x1, blocking collectives, shards(): row_piece = lax.all_gather(normed, 'wide', axis=0, tiled=True)  48.1 us
    psum x1, waiting for transfers between devices, shards(): summed = lax.psum(local_terms, 'narrow')  42.7 us
    all_gather x1, blocking collectives, shards(): every_head = lax.all_gather(heads_out, 'narrow', axis=1, tiled=True)  12.7 us
  transfers between devices with their start and end apart: 4, of which 4 were waited for; matrix products, arithmetic and copies ran while one was open for 1% of the time, Pallas kernels for 0%

commit v1 on v0

--- a/solution.py
+++ b/solution.py
@@ -5,6 +5,13 @@
 from jax.sharding import PartitionSpec as P
 
 D = 7168
+
+
+def swapped_in(shard, mesh_axis, along):
+    devices = lax.axis_size(mesh_axis)
+    blocks = jnp.stack([shard for _ in range(devices)])
+    blocks = lax.all_to_all(blocks, mesh_axis, split_axis=0, concat_axis=0)
+    return jnp.concatenate(blocks, axis=along)
 
 
 def shards(
@@ -68,7 +75,7 @@
         middle * lax.rsqrt(square_sum / D + 1e-06)[:, None] * norm_gain.astype(jnp.float32)
     ).astype(jnp.bfloat16)
     hidden_cols = gate_weight.shape[1]
-    row_piece = lax.all_gather(normed, "wide", axis=0, tiled=True)
+    row_piece = swapped_in(normed, "wide", 0)
     local_terms = jnp.concatenate(
         [
             jnp.dot(row_piece, gate_weight, preferred_element_type=jnp.float32),

time: 593 us -> 567 us (0.956)
  blocking collectives: 123 us -> 96.9 us
    all_gather x1 -> x0, blocking collectives: 48.1 us -> none  [shards(): row_piece = lax.all_gather(normed, 'wide', axis=0, tiled=True)]
    all_to_all x0 -> x1, blocking collectives: none -> 21.8 us  [swapped_in(): blocks = lax.all_to_all(blocks, mesh_axis, split_axis=0, concat_axis=0)]
where the time goes in v1:
time: 567 us; the launch traced here: 566 us
  waiting for transfers between devices  421 us (74%)
  blocking collectives  96.9 us (17%)
  matrix products  16.6 us (3%)
  between operations  13.9 us (2%)
  other arithmetic  9.27 us (2%)
  starting transfers between devices  6.87 us (1%)
    unnamed x5, waiting for transfers between devices  371 us
    all_gather x1, blocking collectives, shards(): gathered = lax.all_gather(packed_queries, 'wide', axis=0, tiled=True)  53.8 us
    psum x1, waiting for transfers between devices, shards(): summed = lax.psum(local_terms, 'narrow')  43 us
    all_to_all x1, blocking collectives, swapped_in(): blocks = lax.all_to_all(blocks, mesh_axis, split_axis=0, concat_axis=0)  21.8 us
    all_gather x1, blocking collectives, shards(): every_head = lax.all_gather(heads_out, 'narrow', axis=1, tiled=True)  12.7 us
  transfers between devices with their start and end apart: 4, of which 4 were waited for; matrix products, arithmetic and copies ran while one was open for 1% of the time, Pallas kernels for 0%

profile of v1, /device:TPU:2, one launch (start us, length us, event | category | flops | bytes accessed | tf_op | source)
XLA Modules:
  0.0 566.4 jit_solution(4672036325003185839)
XLA Ops:
  6.5 0.0 copy-start
  6.5 0.9 compare_and_fusion
  7.4 0.7 pad_maximum_fusion.1
  8.2 53.8 %all_gather.6 = bf16[128,16,192]{2,1,0:T(8,128)(2,1)S(1)} all-gather(bf16[2,16,192]{2,1,0:T(8,128)(2,1)S(1)} %pad_maximum_fusion.1), channel_id=1, replica_groups=mesh['wide'=64,'narrow'=4] {'wide'}, dimensions={0}, use_global_device_ids=true | all-gather | bytes 798720 | tf_op jit(solution)/shard_map/all_gather | solution.py:37
  61.9 0.5 gather_fusion
  62.5 0.1 broadcast_select_fusion
  62.6 0.7 iota_compare_fusion
  63.3 0.0 copy-done
  63.3 0.4 fusion.21
  63.7 3.1 fusion.4
  66.8 0.2 fusion.28
  67.0 3.7 fusion.7
  70.8 0.0 copy-start.4
  70.8 0.0 copy-start.1
  70.8 0.0 copy-start.5
  70.8 0.0 copy-start.2
  70.8 0.0 copy-start.3
  70.8 2.0 fusion.5
  72.8 12.7 %all_gather.7 = bf16[2,64,128]{2,0,1:T(2,128)(2,1)} all-gather(bf16[2,16,128]{2,0,1:T(2,128)(2,1)S(1)} %fusion.5), channel_id=1, replica_groups=mesh['wide'=64,'narrow'=4] {'narrow'}, dimensions={1}, use_global_device_ids=true | all-gather | bytes 40960 | tf_op jit(solution)/shard_map/all_gather | solution.py:60
  85.6 6.7 %all-to-all-start = ((bf16[2,64,128]{2,0,1:T(2,128)(2,1)}), bf16[2,64,128]{2,0,1:T(2,128)(2,1)S(1)}, u32[]{:S(2)}, u32[]{:S(2)}) async-start(bf16[2,64,128]{2,0,1:T(2,128)(2,1)} %all_gather.7), calls=%async_computation | async-start | bytes 65536 | tf_op jit(solution)/shard_map/all_to_all | solution.py:62
  92.3 0.0 all-reduce.8.cloned.1.call-start
  92.4 0.0 copy-done.4
  92.4 2.5 sort.17
  94.9 6.9 %all-to-all-done = bf16[2,64,128]{2,0,1:T(2,128)(2,1)S(1)} async-done(((bf16[2,64,128]{2,0,1:T(2,128)(2,1)}), bf16[2,64,128]{2,0,1:T(2,128)(2,1)S(1)}, u32[]{:S(2)}, u32[]{:S(2)}) %all-to-all-start) | async-done | bytes 32800 | tf_op jit(solution)/shard_map/all_to_all | solution.py:62
  101.8 0.7 gather_fusion.1
  102.5 0.0 copy-done.1
  102.6 1.3 fusion.16
  103.9 0.0 all-reduce.8.cloned.1.call-update
  103.9 0.0 all-reduce.6.cloned.1.call-start
  103.9 0.0 copy-done.5
  103.9 0.6 dynamic-slice
  105.2 180.9 %all-reduce.8.cloned.1.call-done = f32[128,1792]{1,0:T(8,128)} async-done(((f32[128,1792]{1,0:T(8,128)}), f32[128,1792]{1,0:T(8,128)}) %all-reduce.8.cloned.1.call-update) | async-done | bytes 917520
  286.1 0.0 copy-done.2
  286.1 1.0 multiply_reduce_fusion
  287.0 0.0 copy-done.3
  287.0 8.6 %psum.14 = f32[2]{0:T(128)S(1)} all-reduce(f32[2]{0:T(128)S(1)} %multiply_reduce_fusion), channel_id=1, replica_groups=mesh['wide'=64,'narrow'=4] {'narrow'}, use_global_device_ids=true, to_apply=%region_5.6 | all-reduce | flops 2 | bytes 16 | tf_op jit(solution)/shard_map/psum | solution.py:73
  295.6 0.9 multiply_convert_fusion
  296.5 0.2 stack.2
  296.8 21.8 %all_to_all.21 = bf16[64,2,1792]{2,1,0:T(2,128)(2,1)S(1)} all-to-all(bf16[64,2,1792]{2,1,0:T(2,128)(2,1)S(1)} %stack.2), channel_id=1, replica_groups=mesh['wide'=64,'narrow'=4] {'wide'}, dimensions={0} | all-to-all | bytes 917504 | tf_op jit(solution)/shard_map/all_to_all | solution.py:13
  318.6 0.2 reshape.45
  318.7 1.6 fusion.30
  320.4 1.6 fusion.29
  322.0 0.7 pad_maximum_fusion
  322.8 0.0 all-reduce.6.cloned.1.call-update
  322.8 0.0 all-reduce.10.cloned.1.call-start
  322.9 43.0 %all-reduce.6.cloned.1.call-done = f32[128,576]{0,1:T(8,128)} async-done(((f32[128,576]{0,1:T(8,128)}), f32[128,576]{0,1:T(8,128)}) %all-reduce.6.cloned.1.call-update) | async-done | bytes 294928 | tf_op jit(solution)/shard_map/psum | solution.py:86
  365.9 2.8 fusion.9
  368.6 0.0 all-reduce.10.cloned.1.call-update
  368.7 189.7 %all-reduce.10.cloned.1.call-done = f32[128,1792]{1,0:T(8,128)} async-done(((f32[128,1792]{1,0:T(8,128)}), f32[128,1792]{1,0:T(8,128)}) %all-reduce.10.cloned.1.call-update) | async-done | bytes 917520
  558.4 1.5 fusion.20
  (11 shorter events, 0.1 us)
Async XLA Ops:
  6.5 56.8 %copy-start = (bf16[16,128,512]{2,1,0:T(8,128)(2,1)S(1)}, bf16[16,128,512]{2,1,0:T(8,128)(2,1)}, u32[]{:S(2)}) copy-start(bf16[16,128,512]{2,1,0:T(8,128)(2,1)} %param.16) | copy-start | bytes 6291460
  70.8 21.6 %copy-start.4 = (s32[128]{0:T(128)S(1)}, s32[128]{0:T(128)}, u32[]{:S(2)}) copy-start(s32[128]{0:T(128)} %param.20) | copy-start | bytes 1540
  70.8 31.8 %copy-start.1 = (bf16[128,1792]{1,0:T(8,128)(2,1)S(1)}, bf16[128,1792]{1,0:T(8,128)(2,1)}, u32[]{:S(2)}) copy-start(bf16[128,1792]{1,0:T(8,128)(2,1)} %param.21) | copy-start | bytes 1376260
  70.8 33.2 %copy-start.5 = (u32[256]{0:T(256)S(1)}, u32[256]{0:T(256)}, u32[]{:S(2)}) copy-start(u32[256]{0:T(256)} %constant.62) | copy-start | bytes 3076
  70.8 215.3 %copy-start.2 = (bf16[2,1792]{1,0:T(2,128)(2,1)S(1)}, bf16[2,1792]{1,0:T(2,128)(2,1)}, u32[]{:S(2)}) copy-start(bf16[2,1792]{1,0:T(2,128)(2,1)} %param.13) | copy-start | bytes 21508
  70.8 216.2 %copy-start.3 = (bf16[1792]{0:T(1024)(128)(2,1)S(1)}, bf16[1792]{0:T(1024)(128)(2,1)}, u32[]{:S(2)}) copy-start(bf16[1792]{0:T(1024)(128)(2,1)} %param.22) | copy-start | bytes 10756
  85.6 16.3 %all-to-all-start = ((bf16[2,64,128]{2,0,1:T(2,128)(2,1)}), bf16[2,64,128]{2,0,1:T(2,128)(2,1)S(1)}, u32[]{:S(2)}, u32[]{:S(2)}) async-start(bf16[2,64,128]{2,0,1:T(2,128)(2,1)} %all_gather.7), calls=%async_computation | async-start | bytes 65536 | tf_op jit(solution)/shard_map/all_to_all | solution.py:62
  92.3 193.7 %all-reduce.8.cloned.1.call-start = ((), (), s32[]{:S(2)}) async-start(), calls=%async_computation.3 | async-start | bytes 1835008
  103.9 262.0 %all-reduce.6.cloned.1.call-start = ((), (), s32[]{:S(2)}) async-start(), calls=%async_computation.2 | async-start | bytes 589824 | tf_op jit(solution)/shard_map/psum | solution.py:86
  322.8 235.6 %all-reduce.10.cloned.1.call-start = ((), (), s32[]{:S(2)}) async-start(), calls=%async_computation.4 | async-start | bytes 1835008
Sparse Core Ops, SparseCore 0:
  104.0 182.0 all-reduce.7
  322.9 42.8 all-reduce.5
  369.3 189.0 all-reduce.9
